TPU v7x, 256 devices: a whole 4x4x8 slice. The times are simulated.
256 devices in a mesh: wall: 16 (over y, x_lo, core), span: 16 (over x_hi, z).
Axes of the slice: x: 4 (x_hi: 2, x_lo: 2; x = x_hi * 2 + x_lo), y: 4, z: 8, core: 2. Of those that a mesh axis runs over, the one named last changes fastest.
Arguments:
- field: float32 [4, 3, 2, 512, 6144], P(None, None, None, 'wall', 'span'), may hold values from -6 to 6
- mean_flow: float32 [2, 512], P(None, 'wall'), may hold values from 0.2 to 1.5
- d2_coef: float32 [15, 512], P(None, 'wall'), may hold values from -2 to 2
- wall_coef: float32 [2, 8], replicated, may hold values from -0.4375 to 0.4375
- kx_index: int32 [4], replicated, may hold values from 1 to 7
- patch_of: int32 [6144], P('span'), may hold values from 0 to 63
Outputs:
- new_field: float32 [4, 3, 2, 512, 6144], P(None, None, None, 'wall', 'span')
- wall_grad: float32 [2, 4, 2, 64], replicated
All inputs are finite; a program needn't handle non-finite values.
Results may differ from a plain program's by a relative error of at most 0.000073.
Values sent between devices are 32-bit elements; how exact they have to be, the bound alone decides.
A program may use at most 128 MiB of HBM per device.

v0:
```python
import math
import jax
import jax.numpy as jnp
from jax import lax
from jax.sharding import PartitionSpec as P

HALO = 7
STEN = 15
PATCH = 64
TAU = 0.25
VIS = 0.5


def with_halo(block, sides, width):
    for axis, dim in sides:
        count = lax.axis_size(axis)
        forward = [(i, i + 1) for i in range(count - 1)]
        backward = [(target, source) for source, target in forward]
        low = lax.ppermute(
            lax.slice_in_dim(block, block.shape[dim] - width, None, axis=dim), axis, forward
        )
        high = lax.ppermute(lax.slice_in_dim(block, 0, width, axis=dim), axis, backward)
        block = jnp.concatenate([low, block, high], axis=dim)
    return block


def spanwise_operator(line_data):
    item_count, part_count, row_count, length = line_data.shape
    inner_size = 128
    outer_size = length // inner_size
    highest = lax.Precision.HIGHEST
    real_part = line_data[:, 0].reshape(item_count, row_count, outer_size, inner_size)
    imag_part = line_data[:, 1].reshape(item_count, row_count, outer_size, inner_size)
    outer = jnp.arange(outer_size, dtype=jnp.int32)
    inner = jnp.arange(inner_size, dtype=jnp.int32)
    angle_one = (
        -2.0
        * math.pi
        / outer_size
        * (outer[:, None] * outer[None, :] % outer_size).astype(jnp.float32)
    )
    angle_two = (
        -2.0
        * math.pi
        / inner_size
        * (inner[:, None] * inner[None, :] % inner_size).astype(jnp.float32)
    )
    angle_twist = (
        -2.0 * math.pi / length * (outer[:, None] * inner[None, :] % length).astype(jnp.float32)
    )
    cos_one, sin_one = (jnp.cos(angle_one), jnp.sin(angle_one))
    cos_two, sin_two = (jnp.cos(angle_two), jnp.sin(angle_two))
    cos_twist, sin_twist = (jnp.cos(angle_twist), jnp.sin(angle_twist))

    def first_section(table, values):
        return jnp.einsum("kn,irnm->irkm", table, values, precision=highest)

    def second_section(values, table):
        return jnp.einsum("irkn,nm->irkm", values, table, precision=highest)

    def second_back(values, table):
        return jnp.einsum("irkm,nm->irkn", values, table, precision=highest)

    def first_back(table, values):
        return jnp.einsum("kn,irkm->irnm", table, values, precision=highest)

    section_real = first_section(cos_one, real_part) - first_section(sin_one, imag_part)
    section_imag = first_section(cos_one, imag_part) + first_section(sin_one, real_part)
    twist_real = section_real * cos_twist - section_imag * sin_twist
    twist_imag = section_real * sin_twist + section_imag * cos_twist
    modes_real = second_section(twist_real, cos_two) - second_section(twist_imag, sin_two)
    modes_imag = second_section(twist_real, sin_two) + second_section(twist_imag, cos_two)
    wave_index = outer[:, None] + outer_size * inner[None, :]
    signed = jnp.where(wave_index > length // 2, wave_index - length, wave_index)
    cutoff = length // 3
    wave_ratio = signed.astype(jnp.float32) / cutoff
    multiplier = jnp.where(
        jnp.abs(signed) < cutoff, -VIS * wave_ratio * wave_ratio, 0.0 * wave_ratio
    )
    modes_real = modes_real * multiplier
    modes_imag = modes_imag * multiplier
    back_real = second_back(modes_real, cos_two) + second_back(modes_imag, sin_two)
    back_imag = second_back(modes_imag, cos_two) - second_back(modes_real, sin_two)
    untwist_real = back_real * cos_twist + back_imag * sin_twist
    untwist_imag = back_imag * cos_twist - back_real * sin_twist
    result_real = (first_back(cos_one, untwist_real) + first_back(sin_one, untwist_imag)) / length
    result_imag = (first_back(cos_one, untwist_imag) - first_back(sin_one, untwist_real)) / length
    result_real = result_real.reshape(item_count, row_count, length)
    result_imag = result_imag.reshape(item_count, row_count, length)
    return jnp.stack([result_real, result_imag], axis=1)


def on_device(field, mean_flow, d2_coef, wall_coef, kx_index, patch_of):
    mode_count, comp_count, part_count, row_count, col_count = field.shape
    padded = with_halo(field, (("wall", 3),), HALO)
    diffusion = jnp.zeros_like(field)
    for offset in range(STEN):
        diffusion = (
            diffusion + d2_coef[offset][:, None] * padded[:, :, :, offset : offset + row_count, :]
        )
    flattened = field.reshape(mode_count * comp_count, part_count, row_count, col_count)
    spectral_lines = spanwise_operator(
        lax.all_to_all(flattened, "span", split_axis=2, concat_axis=3, tiled=True)
    )
    spanwise = lax.all_to_all(spectral_lines, "span", split_axis=3, concat_axis=2, tiled=True)
    spanwise = spanwise.reshape(field.shape)
    wave_number = kx_index.astype(jnp.float32) * 0.25
    velocity = mean_flow[0]
    shear_rate = mean_flow[1]
    advect_rate = wave_number[:, None, None, None] * velocity[None, None, :, None]
    advect_real = -advect_rate * field[:, :, 1]
    advect_imag = advect_rate * field[:, :, 0]
    advection = jnp.stack([advect_real, advect_imag], axis=2)
    coupling = shear_rate[None, None, :, None] * field[:, 0]
    advection = advection.at[:, 1].add(-coupling)
    new_field = field + TAU * advection + diffusion + spanwise
    lower_wall = jnp.zeros_like(new_field[:, 0, :, 0, :])
    upper_wall = jnp.zeros_like(new_field[:, 0, :, 0, :])
    for offset in range(HALO + 1):
        lower_wall = lower_wall + wall_coef[0, offset] * new_field[:, 0, :, offset, :]
        upper_wall = (
            upper_wall + wall_coef[1, offset] * new_field[:, 0, :, row_count - 1 - offset, :]
        )
    wall_index = lax.axis_index("wall")
    wall_count = lax.axis_size("wall")
    lower_wall = jnp.where(wall_index == 0, lower_wall, 0.0 * lower_wall)
    upper_wall = jnp.where(wall_index == wall_count - 1, upper_wall, 0.0 * upper_wall)
    shear_rows = jnp.stack([lower_wall, upper_wall])
    onehot = (patch_of[:, None] == jnp.arange(PATCH, dtype=jnp.int32)[None, :]).astype(jnp.float32)
    partial_grad = jnp.einsum("wmcz,zp->wmcp", shear_rows, onehot, precision=lax.Precision.HIGHEST)
    wall_grad = lax.psum(partial_grad, ("wall", "span"))
    return (new_field, wall_grad)


def solution(mesh):
    return jax.shard_map(
        on_device,
        mesh=mesh,
        in_specs=(
            P(None, None, None, "wall", "span"),
            P(None, "wall"),
            P(None, "wall"),
            P(),
            P(),
            P("span"),
        ),
        out_specs=(P(None, None, None, "wall", "span"), P()),
        check_vma=False,
    )
```

profile of v0, /device:TPU:1, one launch (start us, length us, event | category | flops | bytes accessed | tf_op | source)
XLA Modules:
  0.0 284.4 jit_solution(1954556570748203936)
XLA Ops:
  0.6 3.2 %copy.115 = f32[4,3,2,32,384]{4,2,1,0,3:T(2,128)} copy(f32[4,3,2,32,384]{4,3,2,1,0:T(8,128)} %param.8) | data formatting | bytes 2359296 | tf_op args[0]
  3.8 11.7 %all-to-all-start = ((f32[12,2,32,384]{3,1,0,2:T(2,128)}), f32[12,2,32,384]{3,1,0,2:T(2,128)S(1)}, u32[]{:S(2)}, u32[]{:S(2)}) async-start(f32[12,2,32,384]{3,1,0,2:T(2,128)} %bitcast.18), calls=%async_computation | async-start | bytes 2359296 | tf_op jit(solution)/shard_map/all_to_all | solution.py:103
  15.6 0.8 copy.109
  16.3 0.9 fusion.198
  17.2 3.0 %collective-permute-start = (f32[4,3,2,7,384]{4,0,2,3,1:T(4,128)}, f32[4,3,2,7,384]{4,0,2,3,1:T(4,128)}, u32[]{:S(2)}, u32[]{:S(2)}) collective-permute-start(f32[4,3,2,7,384]{4,0,2,3,1:T(4,128)} %get-tuple-element.32), channel_id=1, source_target_pairs={{0,16},{16,32},{32,48},{48,64},{64,80},{80,96},{96,112},{112,128},... | collective-permute-start | bytes 774152 | tf_op jit(solution)/shard_map/ppermute | solution.py:19
  20.3 2.0 collective-permute-start.1
  22.3 0.7 fusion.83
  23.0 0.6 multiply_select_fusion
  23.6 21.4 %all-to-all-done = f32[12,2,32,384]{3,1,0,2:T(2,128)S(1)} async-done(((f32[12,2,32,384]{3,1,0,2:T(2,128)}), f32[12,2,32,384]{3,1,0,2:T(2,128)S(1)}, u32[]{:S(2)}, u32[]{:S(2)}) %all-to-all-start) | async-done | bytes 1179680 | tf_op jit(solution)/shard_map/all_to_all | solution.py:103
  45.0 1.4 copy.116
  46.4 2.1 all_to_all.27
  49.1 0.8 fusion.77
  50.4 0.8 fusion.79
  51.1 0.8 convolution_add_fusion.3
  51.9 0.8 convolution_subtract_fusion.3
  52.7 0.9 fusion.24
  53.6 0.9 fusion.26
  54.5 0.9 fusion.4
  55.4 0.9 fusion.40
  56.3 0.9 fusion.5
  57.2 0.9 fusion.43
  58.0 0.9 convolution_subtract_fusion.1
  58.9 0.9 convolution_add_fusion.1
  59.8 0.8 fusion.32
  60.6 1.0 fusion.33
  61.7 0.8 fusion.3
  62.5 4.5 %copy.141 = f32[12,2,48,128]{0,1,3,2:T(2,128)} copy(f32[12,2,48,128]{3,2,1,0:T(8,128)S(1)} %fusion.3) | data formatting | bytes 1179648 | tf_op jit(solution)/shard_map/stack;reshape | solution.py:90
  67.0 1.6 fusion.1
  68.6 4.6 %copy.142 = f32[12,2,48,128]{0,1,3,2:T(2,128)} copy(f32[12,2,48,128]{3,2,1,0:T(8,128)S(1)} %fusion.1) | data formatting | bytes 1179648 | tf_op jit(solution)/shard_map/stack;reshape | solution.py:90
  73.2 11.8 %fusion.200 = f32[6144,2,2,12]{3,2,1,0:T(2,128)} fusion(f32[12,1,2,6144]{0,2,1,3:T(2,128)} %bitcast.155, f32[12,1,2,6144]{0,2,1,3:T(2,128)} %bitcast.154), kind=kLoop, calls=%fused_computation.261 | loop fusion | flops 294912 | bytes 2359296
  85.0 22.7 %reshape.465 = f32[16,1,18432]{2,1,0:T(1,128)} reshape(f32[6144,2,2,12]{3,2,1,0:T(2,128)} %fusion.200) | data formatting | bytes 2359296
  107.7 6.6 %all-to-all-start.1 = ((f32[16,1,18432]{2,1,0:T(1,128)}), f32[16,1,18432]{2,1,0:T(1,128)}, u32[]{:S(2)}, u32[]{:S(2)}) async-start(f32[16,1,18432]{2,1,0:T(1,128)} %reshape.465), calls=%async_computation.1 | async-start | bytes 2359296 | tf_op jit(solution)/shard_map/all_to_all | solution.py:105
  116.5 0.7 fusion.199
  117.3 1.0 fusion.30
  118.3 1.0 copy-done.3
  119.3 1.0 constant_dynamic-update-slice_fusion.1
  120.2 1.0 constant_dynamic-update-slice_fusion
  121.3 1.0 constant_dynamic-update-slice_fusion.2
  122.3 21.7 %all-to-all-done.1 = f32[16,1,18432]{2,1,0:T(1,128)} async-done(((f32[16,1,18432]{2,1,0:T(1,128)}), f32[16,1,18432]{2,1,0:T(1,128)}, u32[]{:S(2)}, u32[]{:S(2)}) %all-to-all-start.1) | async-done | bytes 1179680 | tf_op jit(solution)/shard_map/all_to_all | solution.py:105
  144.5 5.7 %reduce.2 = f32[16,18432]{1,0:T(8,128)} reduce(f32[16,1,18432]{2,1,0:T(1,128)} %all-to-all-done.1, f32[]{:T(128)} %broadcast.394), dimensions={1}, to_apply=%all_to_all.28.reduce_sub_computation | reduce | bytes 2359300 | tf_op jit(solution)/shard_map/all_to_all | solution.py:105
  150.2 27.5 %reshape.466 = f32[6144,2,2,12]{3,2,1,0:T(2,128)} reshape(f32[16,18432]{1,0:T(8,128)} %reduce.2) | data formatting | bytes 2359296
  177.7 11.2 %copy.143 = f32[12,2,2,16,384]{4,3,2,1,0:T(8,128)} copy(f32[12,2,2,16,384]{0,2,1,4,3:T(2,128)} %bitcast.153) | data formatting | bytes 2359296 | tf_op jit(solution)/shard_map/all_to_all | solution.py:105
  188.9 2.3 copy.124
  191.4 4.5 %fusion.8 = f32[4,3,2,32,384]{4,0,2,3,1:T(4,128)S(1)} fusion(f32[4,3,2,39,384]{4,0,2,3,1:T(4,128)S(1)} %constant_dynamic-update-slice_fusion.2, f32[4,3,2,39,384]{4,0,2,3,1:T(4,128)S(1)} %get-tuple-element.30, f32[4,3,2,32,384]{4,2,3,1,0:T(2,128)S(1)} %bitcast.156, f32[4,3,2,32,384]{4,0,2,3,1:T(4,128)S(1)} %copy-done.4, f32[32]{0:T(128)S(1)} %copy-done.19, ...), kind=kLoop, calls=%fused_computation.21 | loop fusion | flops 9732096 | bytes 21235584 | tf_op jit(solution)/shard_map/add | solution.py:116
  195.9 1.2 copy.126
  197.1 5.2 %multiply_select_fusion.1 = f32[1,4,2,384]{3,1,2,0:T(4,128)S(1)} fusion(f32[4,3,2,32,384]{4,0,2,3,1:T(4,128)S(1)} %fusion.8, f32[]{:T(128)} %bitcast.61, f32[]{:T(128)} %bitcast.60, f32[]{:T(128)} %bitcast.59, f32[]{:T(128)} %bitcast.58, f32[]{:T(128)} %bitcast.57, f32[]{:T(128)} %bitcast.56, f32[]{:T(128)} %bitcast.55, f32[]{:T(128)} %bitcast.54, pred[]{:T(512)S(6)} %eq.26), kind=kLoop, calls=%fused_computation.126 | loop fusion | flops 52224 | bytes 110625 | tf_op jit(solution)/shard_map/jit(_where)/select_n | solution.py:127
  202.4 5.1 %multiply_select_fusion.2 = f32[1,4,2,384]{3,1,2,0:T(4,128)S(1)} fusion(f32[4,3,2,32,384]{4,0,2,3,1:T(4,128)S(1)} %fusion.8, f32[]{:T(128)} %bitcast.52, f32[]{:T(128)} %bitcast.51, f32[]{:T(128)} %bitcast.50, f32[]{:T(128)} %bitcast.49, f32[]{:T(128)} %bitcast.48, f32[]{:T(128)} %bitcast.47, f32[]{:T(128)} %bitcast.46, f32[]{:T(128)} %bitcast.45, pred[]{:T(512)S(6)} %eq.25), kind=kLoop, calls=%fused_computation.127 | loop fusion | flops 52224 | bytes 110625 | tf_op jit(solution)/shard_map/jit(_where)/select_n | solution.py:126
  207.7 76.1 %psum.7 = f32[2,4,2,64]{3,1,2,0:T(4,128)S(1)} all-reduce(f32[2,4,2,64]{3,1,2,0:T(4,128)S(1)} %fusion.35), channel_id=1, replica_groups=mesh['wall'=16,'span'=16] {'wall','span'}, use_global_device_ids=true, to_apply=%region_0.1 | all-reduce | flops 1024 | bytes 8192 | tf_op jit(solution)/shard_map/psum | solution.py:131
  (62 shorter events, 4.6 us)
Async XLA Ops:
  3.8 11.7 %copy-start = (f32[4,3,2,32,384]{4,3,2,1,0:T(8,128)S(1)}, f32[4,3,2,32,384]{4,3,2,1,0:T(8,128)}, u32[]{:S(2)}) copy-start(f32[4,3,2,32,384]{4,3,2,1,0:T(8,128)} %param.8) | copy-start | bytes 3538948
  3.8 41.2 %all-to-all-start = ((f32[12,2,32,384]{3,1,0,2:T(2,128)}), f32[12,2,32,384]{3,1,0,2:T(2,128)S(1)}, u32[]{:S(2)}, u32[]{:S(2)}) async-start(f32[12,2,32,384]{3,1,0,2:T(2,128)} %bitcast.18), calls=%async_computation | async-start | bytes 2359296 | tf_op jit(solution)/shard_map/all_to_all | solution.py:103
  17.2 101.0 %collective-permute-start = (f32[4,3,2,7,384]{4,0,2,3,1:T(4,128)}, f32[4,3,2,7,384]{4,0,2,3,1:T(4,128)}, u32[]{:S(2)}, u32[]{:S(2)}) collective-permute-start(f32[4,3,2,7,384]{4,0,2,3,1:T(4,128)} %get-tuple-element.32), channel_id=1, source_target_pairs={{0,16},{16,32},{32,48},{48,64},{64,80},{80,96},{96,112},{112,128},... | collective-permute-start | bytes 774152 | tf_op jit(solution)/shard_map/ppermute | solution.py:19
  20.3 101.0 %collective-permute-start.1 = (f32[4,3,2,7,384]{4,0,2,3,1:T(4,128)}, f32[4,3,2,7,384]{4,0,2,3,1:T(4,128)}, u32[]{:S(2)}, u32[]{:S(2)}) collective-permute-start(f32[4,3,2,7,384]{4,0,2,3,1:T(4,128)} %get-tuple-element.33), channel_id=1, source_target_pairs={{16,0},{32,16},{48,32},{64,48},{80,64},{96,80},{112,96},{128,112},... | collective-permute-start | bytes 774152 | tf_op jit(solution)/shard_map/ppermute | solution.py:22
  51.9 0.8 copy-start.5
  51.9 0.8 copy-start.6
  53.6 0.9 copy-start.7
  107.7 6.7 %copy-start.23 = (s32[4]{0:T(128)S(1)}, s32[4]{0:T(128)}, u32[]{:S(2)}) copy-start(s32[4]{0:T(128)} %param.12) | copy-start | bytes 52
  107.7 6.7 %copy-start.21 = (f32[2,32]{1,0:T(2,128)S(1)}, f32[2,32]{1,0:T(2,128)}, u32[]{:S(2)}) copy-start(f32[2,32]{1,0:T(2,128)} %param.9) | copy-start | bytes 772
  107.7 36.3 %all-to-all-start.1 = ((f32[16,1,18432]{2,1,0:T(1,128)}), f32[16,1,18432]{2,1,0:T(1,128)}, u32[]{:S(2)}, u32[]{:S(2)}) async-start(f32[16,1,18432]{2,1,0:T(1,128)} %reshape.465), calls=%async_computation.1 | async-start | bytes 2359296 | tf_op jit(solution)/shard_map/all_to_all | solution.py:105
  115.2 0.7 copy-start.9
  115.2 1.3 copy-start.8
  117.3 3.0 %copy-start.1 = (f32[4,3,2,32,384]{4,3,2,1,0:T(8,128)S(1)}, f32[4,3,2,32,384]{4,3,2,1,0:T(8,128)}, u32[]{:S(2)}) copy-start(f32[4,3,2,32,384]{4,3,2,1,0:T(8,128)} %param.8) | copy-start | bytes 3538948
  118.2 1.0 copy-start.3
  188.8 2.4 copy-start.2
  188.8 2.4 copy-start.4
  188.8 2.5 copy-start.10
  188.8 2.5 copy-start.11
  188.9 2.5 copy-start.12
  188.9 2.5 copy-start.13
  188.9 2.5 copy-start.14
  188.9 2.5 copy-start.15
  188.9 2.5 copy-start.16
  188.9 2.5 copy-start.17
  188.9 2.5 copy-start.18
  188.9 2.5 copy-start.19
  188.9 2.5 copy-start.20
  195.9 11.6 %copy-start.22 = (s32[384]{0:T(512)S(1)}, s32[384]{0:T(512)}, u32[]{:S(2)}) copy-start(s32[384]{0:T(512)} %param.13) | copy-start | bytes 4612
where the time goes:
time: 286 us; the launch traced here: 284 us
  local copies, waits for them, and re-layouts  90.8 us (32%)
  blocking collectives  76.1 us (27%)
  waiting for transfers between devices  43.1 us (15%)
  other arithmetic  35.3 us (12%)
  starting transfers between devices  23.4 us (8%)
  matrix products  14.5 us (5%)
    psum x1, blocking collectives, on_device(): wall_grad = lax.psum(partial_grad, ('wall', 'span'))  76.1 us
    unnamed x55, local copies, waits for them, and re-layouts  58.4 us
    all_to_all x1, waiting for transfers between devices, on_device(): lax.all_to_all(spectral_lines, 'span', split_axis=3, concat_axis=2, tiled...  21.7 us
    all_to_all x1, waiting for transfers between devices, on_device(): lax.all_to_all(flattened, 'span', split_axis=2, concat_axis=3, tiled=True)  21.4 us
    all_to_all x3, local copies, waits for them, and re-layouts, on_device(): lax.all_to_all(spectral_lines, 'span', split_axis=3, concat_axis=2, tiled...  14 us
    unnamed x1, other arithmetic  11.8 us
    all_to_all x1, starting transfers between devices, on_device(): lax.all_to_all(flattened, 'span', split_axis=2, concat_axis=3, tiled=True)  11.7 us
    another operation x2, local copies, waits for them, and re-layouts, spanwise_operator(): return jnp.stack([result_real, result_imag], axis=1)  9.1 us
  transfers between devices with their start and end apart: 4, of which 2 were waited for; matrix products, arithmetic and copies ran while one was open for 25% of the time, Pallas kernels for 0%

commit v1 on v0

--- a/solution.py
+++ b/solution.py
@@ -128,7 +128,7 @@
     shear_rows = jnp.stack([lower_wall, upper_wall])
     onehot = (patch_of[:, None] == jnp.arange(PATCH, dtype=jnp.int32)[None, :]).astype(jnp.float32)
     partial_grad = jnp.einsum("wmcz,zp->wmcp", shear_rows, onehot, precision=lax.Precision.HIGHEST)
-    wall_grad = lax.psum(partial_grad, ("wall", "span"))
+    wall_grad = jnp.sum(lax.all_gather(partial_grad, ("wall", "span")), axis=0)
     return (new_field, wall_grad)
 
 

time: 286 us -> 920 us (3.22)
  waiting for transfers between devices: 43.1 us -> 734 us
  blocking collectives: 76.1 us -> 0 us
  between operations: 1.24 us -> 14.6 us
    all_gather x0 -> x1, waiting for transfers between devices: none -> 691 us  [on_device(): wall_grad = jnp.sum(lax.all_gather(partial_grad, ('wall', 'span')), axis=0)]
    psum x1 -> x0, blocking collectives: 76.1 us -> none  [on_device(): wall_grad = lax.psum(partial_grad, ('wall', 'span'))]
    unnamed x55 -> x57, local copies, waits for them, and re-layouts: 58.4 us -> 59.7 us
  transfers between devices with their start and end apart: 4 -> 5, of which waited for: 2 -> 3; matrix products, arithmetic and copies ran while one was open for 25% -> 8% of each run, Pallas kernels for 0% -> 0%
where the time goes in v1:
time: 920 us; the launch traced here: 917 us
  waiting for transfers between devices  734 us (80%)
  local copies, waits for them, and re-layouts  92.1 us (10%)
  other arithmetic  37.3 us (4%)
  starting transfers between devices  23.4 us (3%)
  matrix products  15.1 us (2%)
  between operations  14.6 us (2%)
    all_gather x1, waiting for transfers between devices, on_device(): wall_grad = jnp.sum(lax.all_gather(partial_grad, ('wall', 'span')), axis=0)  691 us
    unnamed x57, local copies, waits for them, and re-layouts  59.7 us
    all_to_all x1, waiting for transfers between devices, on_device(): lax.all_to_all(spectral_lines, 'span', split_axis=3, concat_axis=2, tiled...  21.6 us
    all_to_all x1, waiting for transfers between devices, on_device(): lax.all_to_all(flattened, 'span', split_axis=2, concat_axis=3, tiled=True)  21.4 us
  transfers between devices with their start and end apart: 5, of which 3 were waited for; matrix products, arithmetic and copies ran while one was open for 8% of the time, Pallas kernels for 0%

profile of v1, /device:TPU:1, one launch (start us, length us, event | category | flops | bytes accessed | tf_op | source)
XLA Modules:
  0.0 916.5 jit_solution(1270246264563269594)
XLA Ops:
  7.2 3.2 copy.112
  10.4 11.7 %all-to-all-start = ((f32[12,2,32,384]{3,1,0,2:T(2,128)}), f32[12,2,32,384]{3,1,0,2:T(2,128)S(1)}, u32[]{:S(2)}, u32[]{:S(2)}) async-start(f32[12,2,32,384]{3,1,0,2:T(2,128)} %bitcast.18), calls=%async_computation | async-start | bytes 2359296 | tf_op jit(solution)/shard_map/all_to_all | solution.py:103
  22.1 0.8 copy.106
  22.9 0.9 fusion.198
  23.7 3.0 collective-permute-start
  26.8 1.9 collective-permute-start.1
  28.8 0.8 fusion.83
  30.1 21.4 %all-to-all-done = f32[12,2,32,384]{3,1,0,2:T(2,128)S(1)} async-done(((f32[12,2,32,384]{3,1,0,2:T(2,128)}), f32[12,2,32,384]{3,1,0,2:T(2,128)S(1)}, u32[]{:S(2)}, u32[]{:S(2)}) %all-to-all-start) | async-done | bytes 1179680 | tf_op jit(solution)/shard_map/all_to_all | solution.py:103
  51.6 1.4 copy.113
  53.0 2.1 all_to_all.27
  55.6 0.8 fusion.77
  56.9 0.8 fusion.79
  57.7 0.8 convolution_add_fusion.3
  58.5 0.8 convolution_subtract_fusion.3
  59.3 0.9 fusion.24
  60.2 0.9 fusion.26
  61.1 0.9 fusion.4
  61.9 0.9 fusion.40
  62.8 0.9 fusion.5
  63.7 0.9 fusion.43
  64.6 0.9 convolution_subtract_fusion.1
  65.5 0.9 convolution_add_fusion.1
  66.3 0.8 fusion.32
  67.2 1.0 fusion.33
  68.2 0.8 fusion.3
  69.1 4.5 copy.138
  73.5 1.6 fusion.1
  75.1 4.6 copy.139
  79.7 11.8 %fusion.200 = f32[6144,2,2,12]{3,2,1,0:T(2,128)} fusion(f32[12,1,2,6144]{0,2,1,3:T(2,128)} %bitcast.156, f32[12,1,2,6144]{0,2,1,3:T(2,128)} %bitcast.155), kind=kLoop, calls=%fused_computation.261 | loop fusion | flops 294912 | bytes 2359296
  91.5 22.7 %reshape.466 = f32[16,1,18432]{2,1,0:T(1,128)} reshape(f32[6144,2,2,12]{3,2,1,0:T(2,128)} %fusion.200) | data formatting | bytes 2359296
  114.2 6.6 all-to-all-start.1
  123.8 1.0 fusion.30
  124.8 1.0 copy-done.4
  125.8 1.0 constant_dynamic-update-slice_fusion.1
  126.8 1.0 constant_dynamic-update-slice_fusion
  127.9 1.0 constant_dynamic-update-slice_fusion.2
  128.9 21.6 %all-to-all-done.1 = f32[16,1,18432]{2,1,0:T(1,128)} async-done(((f32[16,1,18432]{2,1,0:T(1,128)}), f32[16,1,18432]{2,1,0:T(1,128)}, u32[]{:S(2)}, u32[]{:S(2)}) %all-to-all-start.1) | async-done | bytes 1179680 | tf_op jit(solution)/shard_map/all_to_all | solution.py:105
  151.0 5.7 reduce.2
  156.7 27.5 %reshape.467 = f32[6144,2,2,12]{3,2,1,0:T(2,128)} reshape(f32[16,18432]{1,0:T(8,128)} %reduce.2) | data formatting | bytes 2359296
  184.2 11.2 %copy.140 = f32[12,2,2,16,384]{4,3,2,1,0:T(8,128)} copy(f32[12,2,2,16,384]{0,2,1,4,3:T(2,128)} %bitcast.154) | data formatting | bytes 2359296 | tf_op jit(solution)/shard_map/all_to_all | solution.py:105
  195.5 2.3 copy.121
  197.9 4.5 fusion.8
  202.4 5.2 multiply_select_fusion.1
  207.6 5.1 multiply_select_fusion.2
  212.8 0.8 fusion.35
  213.6 2.5 copy.123
  216.1 690.9 %all-gather.3.cloned.1.call-done = f32[512,4,2,64]{3,1,2,0:T(4,128)} async-done(((f32[2,4,2,64]{3,1,2,0:T(4,128)}), f32[512,4,2,64]{3,1,2,0:T(4,128)}) %all-gather.3.cloned.1.call-update) | async-done | bytes 1048592 | tf_op jit(solution)/shard_map/all_gather | solution.py:131
  907.0 2.1 reduce_sum.9
  (67 shorter events, 5.8 us)
Async XLA Ops:
  10.4 11.7 %copy-start = (f32[4,3,2,32,384]{4,3,2,1,0:T(8,128)S(1)}, f32[4,3,2,32,384]{4,3,2,1,0:T(8,128)}, u32[]{:S(2)}) copy-start(f32[4,3,2,32,384]{4,3,2,1,0:T(8,128)} %param.8) | copy-start | bytes 3538948
  10.4 41.2 %all-to-all-start = ((f32[12,2,32,384]{3,1,0,2:T(2,128)}), f32[12,2,32,384]{3,1,0,2:T(2,128)S(1)}, u32[]{:S(2)}, u32[]{:S(2)}) async-start(f32[12,2,32,384]{3,1,0,2:T(2,128)} %bitcast.18), calls=%async_computation | async-start | bytes 2359296 | tf_op jit(solution)/shard_map/all_to_all | solution.py:103
  23.7 101.1 %collective-permute-start = (f32[4,3,2,7,384]{4,0,2,3,1:T(4,128)}, f32[4,3,2,7,384]{4,0,2,3,1:T(4,128)}, u32[]{:S(2)}, u32[]{:S(2)}) collective-permute-start(f32[4,3,2,7,384]{4,0,2,3,1:T(4,128)} %get-tuple-element.32), channel_id=1, source_target_pairs={{0,16},{16,32},{32,48},{48,64},{64,80},{80,96},{96,112},{112,128},... | collective-permute-start | bytes 774152 | tf_op jit(solution)/shard_map/ppermute | solution.py:19
  26.8 101.1 %collective-permute-start.1 = (f32[4,3,2,7,384]{4,0,2,3,1:T(4,128)}, f32[4,3,2,7,384]{4,0,2,3,1:T(4,128)}, u32[]{:S(2)}, u32[]{:S(2)}) collective-permute-start(f32[4,3,2,7,384]{4,0,2,3,1:T(4,128)} %get-tuple-element.33), channel_id=1, source_target_pairs={{16,0},{32,16},{48,32},{64,48},{80,64},{96,80},{112,96},{128,112},... | collective-permute-start | bytes 774152 | tf_op jit(solution)/shard_map/ppermute | solution.py:22
  58.5 0.8 copy-start.6
  58.5 0.8 copy-start.7
  60.2 0.9 copy-start.8
  114.2 6.7 copy-start.24
  114.2 6.7 copy-start.22
  114.2 36.3 %all-to-all-start.1 = ((f32[16,1,18432]{2,1,0:T(1,128)}), f32[16,1,18432]{2,1,0:T(1,128)}, u32[]{:S(2)}, u32[]{:S(2)}) async-start(f32[16,1,18432]{2,1,0:T(1,128)} %reshape.466), calls=%async_computation.1 | async-start | bytes 2359296 | tf_op jit(solution)/shard_map/all_to_all | solution.py:105
  120.8 786.1 %all-gather.3.cloned.1.call-start = ((), (), s32[]{:S(2)}) async-start(), calls=%async_computation.2 | async-start | bytes 2105344 | tf_op jit(solution)/shard_map/all_gather | solution.py:131
  121.8 0.7 copy-start.10
  121.8 1.3 copy-start.9
  123.8 3.0 copy-start.1
  124.8 1.0 copy-start.4
  195.4 2.4 copy-start.2
  195.4 2.4 copy-start.5
  195.4 2.5 copy-start.11
  195.4 2.5 copy-start.12
  195.4 2.5 copy-start.13
  195.4 2.5 copy-start.14
  195.4 2.5 copy-start.15
  195.4 2.5 copy-start.16
  195.4 2.5 copy-start.17
  195.4 2.5 copy-start.18
  195.4 2.5 copy-start.19
  195.4 2.5 copy-start.20
  195.4 2.5 copy-start.21
  197.9 14.8 %copy-start.23 = (s32[384]{0:T(512)S(1)}, s32[384]{0:T(512)}, u32[]{:S(2)}) copy-start(s32[384]{0:T(512)} %param.13) | copy-start | bytes 4612
  202.4 5.2 copy-start.3
Sparse Core Ops, SparseCore 0:
  213.7 693.2 all-gather.2
